TPU v7x, 128 devices: a whole 4x4x4 slice. The times are simulated.
128 devices in a mesh: cent: 4 (over y), rows: 32 (over z, x, core).
Axes of the slice: x: 4, y: 4, z: 4, core: 2. Of those that a mesh axis runs over, the one named last changes fastest.
Arguments:
- embeddings: bfloat16 [32768, 2048], P(('cent', 'rows')), may hold values from -6 to 6
- centroids: bfloat16 [16384, 2048], P(('cent', 'rows')), may hold values from -0.125 to 0.125
- cluster: int32 [32768, 1], P(('cent', 'rows')), may hold values from 0 to 127; in each aligned block of 256 rows (0 to 255, 256 to 511, ...) at most 4 rows name the same one
- noise_salt: int32 [1], replicated, may hold values from 0 to 1048575
Outputs:
- perturbed_max: float32 [32768], P(('cent', 'rows'))
- dedup_score: float32 [32768], P(('cent', 'rows'))
- new_centroids: float32 [128, 2048], P(('cent', 'rows'))
Inputs may be any that keep to these rules, and one draw needn't show every extreme that they name: In every aligned block of 256 rows (the rows of one device) no cluster is named by more than 4 rows, and in some block some cluster by exactly 4; every cluster is named by some row.
All inputs are finite; a program needn't handle non-finite values.
Results may differ from a plain program's by a relative error of at most 0.0003.
Values may be sent and summed in bfloat16 or wider, within the bound.
A program may use at most 128 MiB of HBM per device.

v0:
```python
import math
import jax
import jax.numpy as jnp
from jax import lax
from jax.sharding import Mesh
from jax.sharding import PartitionSpec as P

inverse_temp = 3.0
epsilon = 1e-06
ALL = ("y", "z", "x", "c")


def logical_shift(word, amount):
    return lax.shift_right_logical(word, jnp.full(word.shape, amount, jnp.int32))


def gumbel_noise(row_ids, cent_ids, salt_word):
    mixed = row_ids * 1103515245 + cent_ids * 739982445 + salt_word
    mixed = mixed ^ logical_shift(mixed, 16)
    mixed = mixed * 2146121005
    mixed = mixed ^ logical_shift(mixed, 15)
    mixed = mixed * 1759714725
    mixed = mixed ^ logical_shift(mixed, 16)
    low_bits = mixed & 8388607
    uniform = (low_bits.astype(jnp.float32) + 0.5) * (1.0 / 8388608.0)
    return -jnp.log(-jnp.log(uniform))


def cluster_stats(members, valid):
    feature_dim = members.shape[1]
    widened = members.astype(jnp.float32)
    scale = lax.rsqrt(jnp.mean(widened * widened, axis=1) + epsilon)
    gram = lax.dot_general(
        members, members, (((1,), (1,)), ((), ())), preferred_element_type=jnp.float32
    )
    similar = gram * scale[:, None] * scale[None, :] * (1.0 / math.sqrt(feature_dim))
    order = jnp.arange(members.shape[0], dtype=jnp.int32)
    usable = valid[None, :] & (order[:, None] != order[None, :])
    highest = jnp.max(jnp.where(usable, similar, -1e30), axis=1)
    scores = jnp.where(jnp.any(usable, axis=1), highest, 0.0)
    total = jnp.sum(jnp.where(valid[:, None], widened, 0.0), axis=0)
    center = total * lax.rsqrt(jnp.mean(total * total) + epsilon)
    return (scores, center)


def shards(embeddings, centroids, cluster, noise_salt):
    rows_dev, feature_dim = embeddings.shape
    cent_dev = centroids.shape[0]
    ny, nz, nx, nc = (lax.axis_size(a) for a in ALL)
    devices = ny * nz * nx * nc
    capacity = max(2, 2 * rows_dev // devices)
    iy, iz, ix, ic = (lax.axis_index(a) for a in ALL)
    me = ((iy * nz + iz) * nx + ix) * nc + ic
    salt_word = noise_salt[0]
    group = lax.all_gather(
        lax.all_gather(embeddings, "y", axis=0, tiled=True), "c", axis=0, tiled=True
    )
    piece = lax.all_gather(centroids, ("z", "x"), axis=0, tiled=True)
    position = jnp.arange(nc * ny * rows_dev, dtype=jnp.int32)
    src_c = position // (ny * rows_dev)
    src_y = position // rows_dev % ny
    row_dev = ((src_y * nz + iz) * nx + ix) * nc + src_c
    group_ids = row_dev * rows_dev + position % rows_dev
    cpos = jnp.arange(nz * nx * cent_dev, dtype=jnp.int32)
    cent_dev_ids = ((iy * nz + cpos // (nx * cent_dev)) * nx + cpos // cent_dev % nx) * nc + ic
    cent_ids = cent_dev_ids * cent_dev + cpos % cent_dev
    piece_rows = piece.shape[0]
    block = math.gcd(piece_rows, 512)
    steps = piece_rows // block
    tiles = piece.reshape(steps, block, feature_dim)
    noise = gumbel_noise(group_ids[:, None], cent_ids[None, :], salt_word)
    noise_tiles = noise.reshape(group.shape[0], steps, block).transpose(1, 0, 2)
    initial = jnp.full((group.shape[0],), -1e30, jnp.float32)

    def step(carry, item):
        tile, noise_tile = item
        scores = lax.dot_general(
            group, tile, (((1,), (1,)), ((), ())), preferred_element_type=jnp.float32
        )
        perturbed = inverse_temp * scores + noise_tile
        return (jnp.maximum(carry, jnp.max(perturbed, axis=1)), None)

    result, unused = lax.scan(step, initial, (tiles, noise_tiles))
    merged = lax.pmax(result, ("c", "y"))
    perturbed_max = lax.dynamic_slice_in_dim(merged, (ic * ny + iy) * rows_dev, rows_dev)
    assigned = cluster[:, 0]
    order = jnp.arange(rows_dev, dtype=jnp.int32)
    same = (assigned[:, None] == assigned[None, :]) & (order[None, :] < order[:, None])
    rank = jnp.sum(same.astype(jnp.int32), axis=1)
    slot = assigned * capacity + rank
    outgoing = jnp.zeros((devices * capacity, feature_dim), jnp.bfloat16).at[slot].set(embeddings)
    present = (
        jnp.zeros((devices * capacity,), jnp.bfloat16)
        .at[slot]
        .set(jnp.ones((rows_dev,), jnp.bfloat16))
    )
    received = lax.all_to_all(
        outgoing.reshape(devices, capacity, feature_dim),
        ALL,
        split_axis=0,
        concat_axis=0,
        tiled=True,
    )
    arrived = lax.all_to_all(
        present.reshape(devices, capacity), ALL, split_axis=0, concat_axis=0, tiled=True
    )
    members = received.reshape(devices * capacity, feature_dim)
    valid = arrived.reshape(devices * capacity) > 0.5
    scores, center = cluster_stats(members, valid)
    returned = lax.all_to_all(
        scores.reshape(devices, capacity), ALL, split_axis=0, concat_axis=0, tiled=True
    )
    dedup_score = returned.reshape(devices * capacity)[slot]
    return (perturbed_max, dedup_score, center[None, :])


def solution(mesh):
    cent_count, rows_count = mesh.devices.shape
    cores = 2
    side = math.isqrt(rows_count // cores)
    view = Mesh(mesh.devices.reshape(cent_count, side, rows_count // cores // side, cores), ALL)
    spec = P(ALL, None)
    in_specs = (spec, spec, spec, P())
    out_specs = (P(ALL), P(ALL), spec)
    return jax.shard_map(shards, mesh=view, in_specs=in_specs, out_specs=out_specs, check_vma=False)
```

profile of v0, /device:TPU:1, one launch (start us, length us, event | category | flops | bytes accessed | tf_op | source)
XLA Modules:
  0.0 235.4 jit_solution(165970841655316677)
XLA Ops:
  7.2 0.0 all-gather.6.cloned.1.call-start
  7.2 0.7 all-gather.6.cloned.1.call-update
  7.9 0.0 all-gather.8.cloned.1.call-start
  7.9 53.2 %all-gather.6.cloned.1.call-done = bf16[1024,2048]{1,0:T(8,128)(2,1)} async-done(((bf16[256,2048]{1,0:T(8,128)(2,1)}), bf16[1024,2048]{1,0:T(8,128)(2,1)}) %all-gather.6.cloned.1.call-update) | async-done | bytes 4194320 | tf_op jit(solution)/shard_map/all_gather | solution.py:56
  61.2 0.0 all-gather.8.cloned.1.call-update
  61.2 0.0 all-gather.4.cloned.1.call-start
  61.3 0.7 all-gather.4.cloned.1.call-update
  62.0 0.9 convert_reduce_fusion
  62.9 0.7 compare_select_fusion
  63.6 2.2 scatter_custom_fusion
  65.7 0.8 all_to_all.17
  66.5 8.6 %all-to-all-start = ((bf16[128,1,4]{2,1,0:T(2,128)(2,1)}), bf16[128,1,4]{2,1,0:T(2,128)(2,1)S(1)}, u32[]{:S(2)}, u32[]{:S(2)}) async-start(bf16[128,1,4]{2,1,0:T(2,128)(2,1)} %all_to_all.17), calls=%async_computation | async-start | bytes 131072 | tf_op jit(solution)/shard_map/all_to_all | solution.py:104
  75.2 3.7 %scatter_custom_fusion.1 = bf16[512,2048]{1,0:T(8,128)(2,1)S(1)} fusion(s32[256]{0:T(256)S(1)} %bitcast.33, bf16[256,2048]{1,0:T(8,128)(2,1)} %param.6, bf16[]{:T(256)} %constant.177.clone.1), kind=kCustom, calls=%fused_computation.31 | custom fusion | bytes 2097664 | tf_op jit(solution)/shard_map/scatter | solution.py:91
  79.6 2.2 reshape.217
  81.8 2.8 %all-to-all-done = bf16[128,1,4]{2,1,0:T(2,128)(2,1)S(1)} async-done(((bf16[128,1,4]{2,1,0:T(2,128)(2,1)}), bf16[128,1,4]{2,1,0:T(2,128)(2,1)S(1)}, u32[]{:S(2)}, u32[]{:S(2)}) %all-to-all-start) | async-done | bytes 1056 | tf_op jit(solution)/shard_map/all_to_all | solution.py:104
  84.6 6.9 %all-to-all-start.1 = ((bf16[128,4,2048]{2,1,0:T(4,128)(2,1)}), bf16[128,4,2048]{2,1,0:T(4,128)(2,1)S(1)}, u32[]{:S(2)}, u32[]{:S(2)}) async-start(bf16[128,4,2048]{2,1,0:T(4,128)(2,1)} %reshape.217), calls=%async_computation.1 | async-start | bytes 4194304 | tf_op jit(solution)/shard_map/all_to_all | solution.py:97
  91.5 12.2 %fusion.13 = f32[4,2048,512]{1,2,0:T(8,128)} fusion(s32[]{:T(128)} %bitcast.28, s32[4,512]{1,0:T(4,128)S(1)} %fusion.55, s32[2048]{0:T(1024)S(1)} %fusion.40), kind=kLoop, calls=%fused_computation.21 | loop fusion | flops 67108864 | bytes 16793604 | tf_op jit(solution)/shard_map/neg | solution.py:26
  103.7 0.3 broadcast_compare_fusion
  104.0 0.1 copy.15
  104.1 0.1 copy.16
  104.2 0.1 gt.22
  104.4 0.2 fusion.23
  104.5 25.5 %all-to-all-done.1 = bf16[128,4,2048]{2,1,0:T(4,128)(2,1)S(1)} async-done(((bf16[128,4,2048]{2,1,0:T(4,128)(2,1)}), bf16[128,4,2048]{2,1,0:T(4,128)(2,1)S(1)}, u32[]{:S(2)}, u32[]{:S(2)}) %all-to-all-start.1) | async-done | bytes 2097184 | tf_op jit(solution)/shard_map/all_to_all | solution.py:97
  130.0 2.1 fusion.15
  132.1 0.1 rsqrt.18
  132.2 2.0 reshape.218
  134.3 4.3 %fusion.19 = f32[512]{0:T(512)S(1)} fusion(bf16[512,2048]{1,0:T(8,128)(2,1)} %reshape.218, f32[512]{0:T(512)S(1)} %rsqrt.18, pred[512]{0:T(512)(128)(4,1)S(1)} %gt.22), kind=kOutput, calls=%fused_computation.30 | convolution fusion | flops 1075576320 | bytes 2101760 | tf_op jit(solution)/shard_map/dot_general | solution.py:33
  138.6 0.7 select_n.110
  139.3 4.5 %all-to-all-start.2 = ((f32[128,1,4]{2,1,0:T(1,128)}), f32[128,1,4]{2,1,0:T(1,128)S(1)}, u32[]{:S(2)}, u32[]{:S(2)}) async-start(f32[128,1,4]{2,1,0:T(1,128)} %bitcast.5), calls=%async_computation.2 | async-start | bytes 131072 | tf_op jit(solution)/shard_map/all_to_all | solution.py:110
  143.8 0.6 multiply_reduce_fusion
  145.1 0.6 broadcast_multiply_fusion
  145.7 8.0 %all-to-all-done.2 = f32[128,1,4]{2,1,0:T(1,128)S(1)} async-done(((f32[128,1,4]{2,1,0:T(1,128)}), f32[128,1,4]{2,1,0:T(1,128)S(1)}, u32[]{:S(2)}, u32[]{:S(2)}) %all-to-all-start.2) | async-done | bytes 2080 | tf_op jit(solution)/shard_map/all_to_all | solution.py:110
  153.7 0.5 broadcast.395
  154.3 0.8 reduce.7
  155.1 0.1 reshape.219
  155.2 2.5 %gather_fusion = f32[256]{0:T(256)} fusion(f32[512]{0:T(512)S(1)} %reshape.219, s32[1024]{0:T(1024)S(1)} %pad_clamp_fusion), kind=kCustom, calls=%fused_computation | custom fusion | bytes 3072 | tf_op jit(solution)/shard_map/gather | solution.py:113
  157.7 0.0 all-gather.8.cloned.1.call-done
  157.7 15.8 %all-gather.4.cloned.1.call-done = bf16[2048,2048]{1,0:T(8,128)(2,1)} async-done(((bf16[128,2048]{1,0:T(8,128)(2,1)}), bf16[2048,2048]{1,0:T(8,128)(2,1)}) %all-gather.4.cloned.1.call-update) | async-done | bytes 8388624 | tf_op jit(solution)/shard_map/all_gather | solution.py:58
  173.5 39.0 %while.11 = (s32[]{:T(128)}, f32[2048]{0:T(1024)S(1)}, bf16[4,512,2048]{2,1,0:T(8,128)(2,1)}, bf16[2048,2048]{1,0:T(8,128)(2,1)}, f32[4,2048,512]{1,2,0:T(8,128)}, /*index=5*/s32[]{:T(128)}, s32[]{:T(128)}) while((s32[]{:T(128)}, f32[2048]{0:T(1024)S(1)}, bf16[4,512,2048]{2,1,0:T(8,128)(2,1)}, bf16[2048,2048]{1,0:T(8,128)(2,1)}, ...), condition=%wide.region_2.3_spmd.clone, body=%wide.region_0.2_spmd.clone.sunk | while | flops 4298115072 | bytes 14713943 | solution.py:83
  173.5 9.7 %fusion.69 = f32[2048]{0:T(1024)S(1)} fusion(f32[4,2048,512]{1,2,0:T(8,128)} %get-tuple-element.112, s32[]{:T(128)} %get-tuple-element.101, bf16[2048,2048]{1,0:T(8,128)(2,1)} %get-tuple-element.111, bf16[4,512,2048]{2,1,0:T(8,128)(2,1)} %get-tuple-element.110), kind=kOutput, calls=%fused_computation.4.clone.1 | convolution fusion | flops 4298110976 | bytes 14689280 | tf_op jit(solution)/shard_map/while/body/eval_jaxpr/dot_general | solution.py:77
  183.2 9.7 %fusion.69 = f32[2048]{0:T(1024)S(1)} fusion(f32[4,2048,512]{1,2,0:T(8,128)} %get-tuple-element.112, s32[]{:T(128)} %get-tuple-element.101, bf16[2048,2048]{1,0:T(8,128)(2,1)} %get-tuple-element.111, bf16[4,512,2048]{2,1,0:T(8,128)(2,1)} %get-tuple-element.110), kind=kOutput, calls=%fused_computation.4.clone.1 | convolution fusion | flops 4298110976 | bytes 14689280 | tf_op jit(solution)/shard_map/while/body/eval_jaxpr/dot_general | solution.py:77
  193.0 9.7 %fusion.69 = f32[2048]{0:T(1024)S(1)} fusion(f32[4,2048,512]{1,2,0:T(8,128)} %get-tuple-element.112, s32[]{:T(128)} %get-tuple-element.101, bf16[2048,2048]{1,0:T(8,128)(2,1)} %get-tuple-element.111, bf16[4,512,2048]{2,1,0:T(8,128)(2,1)} %get-tuple-element.110), kind=kOutput, calls=%fused_computation.4.clone.1 | convolution fusion | flops 4298110976 | bytes 14689280 | tf_op jit(solution)/shard_map/while/body/eval_jaxpr/dot_general | solution.py:77
  202.7 9.7 %fusion.69 = f32[2048]{0:T(1024)S(1)} fusion(f32[4,2048,512]{1,2,0:T(8,128)} %get-tuple-element.112, s32[]{:T(128)} %get-tuple-element.101, bf16[2048,2048]{1,0:T(8,128)(2,1)} %get-tuple-element.111, bf16[4,512,2048]{2,1,0:T(8,128)(2,1)} %get-tuple-element.110), kind=kOutput, calls=%fused_computation.4.clone.1 | convolution fusion | flops 4298110976 | bytes 14689280 | tf_op jit(solution)/shard_map/while/body/eval_jaxpr/dot_general | solution.py:77
  212.5 15.8 %pmax.7 = f32[2048]{0:T(1024)S(1)} all-reduce(f32[2048]{0:T(1024)S(1)} %get-tuple-element.30), channel_id=1, replica_groups=mesh['y'=4,'z'=4,'x'=4,'c'=2] {'c','y'}, use_global_device_ids=true, to_apply=%region_3.4 | all-reduce | flops 2048 | bytes 16384 | tf_op jit(solution)/shard_map/pmax | solution.py:84
  228.2 0.6 dynamic_slice.11
  (11 shorter events, 0.1 us)
Async XLA Ops:
  7.2 54.0 %all-gather.6.cloned.1.call-start = ((), (), s32[]{:S(2)}) async-start(), calls=%async_computation.4 | async-start | bytes 5242880 | tf_op jit(solution)/shard_map/all_gather | solution.py:56
  7.9 149.8 %all-gather.8.cloned.1.call-start = ((), (), s32[]{:S(2)}) async-start(), calls=%async_computation.5 | async-start | bytes 12582912 | tf_op jit(solution)/shard_map/all_gather | solution.py:55
  61.2 112.3 %all-gather.4.cloned.1.call-start = ((), (), s32[]{:S(2)}) async-start(), calls=%async_computation.3 | async-start | bytes 8912896 | tf_op jit(solution)/shard_map/all_gather | solution.py:58
  66.5 18.1 %all-to-all-start = ((bf16[128,1,4]{2,1,0:T(2,128)(2,1)}), bf16[128,1,4]{2,1,0:T(2,128)(2,1)S(1)}, u32[]{:S(2)}, u32[]{:S(2)}) async-start(bf16[128,1,4]{2,1,0:T(2,128)(2,1)} %all_to_all.17), calls=%async_computation | async-start | bytes 131072 | tf_op jit(solution)/shard_map/all_to_all | solution.py:104
  84.6 45.4 %all-to-all-start.1 = ((bf16[128,4,2048]{2,1,0:T(4,128)(2,1)}), bf16[128,4,2048]{2,1,0:T(4,128)(2,1)S(1)}, u32[]{:S(2)}, u32[]{:S(2)}) async-start(bf16[128,4,2048]{2,1,0:T(4,128)(2,1)} %reshape.217), calls=%async_computation.1 | async-start | bytes 4194304 | tf_op jit(solution)/shard_map/all_to_all | solution.py:97
  139.3 14.4 %all-to-all-start.2 = ((f32[128,1,4]{2,1,0:T(1,128)}), f32[128,1,4]{2,1,0:T(1,128)S(1)}, u32[]{:S(2)}, u32[]{:S(2)}) async-start(f32[128,1,4]{2,1,0:T(1,128)} %bitcast.5), calls=%async_computation.2 | async-start | bytes 131072 | tf_op jit(solution)/shard_map/all_to_all | solution.py:110
Sparse Core Ops, SparseCore 0:
  9.7 51.4 all-gather.5
  62.8 23.2 all-gather.7
  88.3 85.1 all-gather.3
where the time goes:
time: 236 us; the launch traced here: 235 us
  waiting for transfers between devices  107 us (45%)
  matrix products  43.1 us (18%)
  starting transfers between devices  20.1 us (9%)
  other arithmetic  18.5 us (8%)
  local copies, waits for them, and re-layouts  15.8 us (7%)
  blocking collectives  15.8 us (7%)
  between operations  15.2 us (6%)
    all_gather x1, waiting for transfers between devices, shards(): lax.all_gather(embeddings, 'y', axis=0, tiled=True)  53.2 us
    dot_general x4, matrix products, step(): lax.dot_general(group, tile, (((1,), (1,)), ((), ())), preferred_element_...  38.8 us
    all_to_all x1, waiting for transfers between devices, shards(): lax.all_to_all(outgoing.reshape(devices, capacity, feature_dim), ALL, spl...  25.5 us
    all_gather x1, waiting for transfers between devices, shards(): piece = lax.all_gather(centroids, ('z', 'x'), axis=0, tiled=True)  15.8 us
    pmax x1, blocking collectives, shards(): merged = lax.pmax(result, ('c', 'y'))  15.8 us
    neg x1, other arithmetic, gumbel_noise(): return -jnp.log(-jnp.log(uniform))  12.2 us
    all_to_all x1, starting transfers between devices, shards(): lax.all_to_all(present.reshape(devices, capacity), ALL, split_axis=0, con...  8.6 us
    all_to_all x1, waiting for transfers between devices, shards(): lax.all_to_all(scores.reshape(devices, capacity), ALL, split_axis=0, conc...  8.01 us
  transfers between devices with their start and end apart: 6, of which 5 were waited for; matrix products, arithmetic and copies ran while one was open for 16% of the time, Pallas kernels for 0%

commit v1 on v0

--- a/solution.py
+++ b/solution.py
@@ -55,7 +55,9 @@
     group = lax.all_gather(
         lax.all_gather(embeddings, "y", axis=0, tiled=True), "c", axis=0, tiled=True
     )
-    piece = lax.all_gather(centroids, ("z", "x"), axis=0, tiled=True)
+    piece = jnp.concatenate(
+        lax.all_to_all(jnp.stack([centroids] * lax.axis_size(("z", "x"))), ("z", "x"), 0, 0), axis=0
+    )
     position = jnp.arange(nc * ny * rows_dev, dtype=jnp.int32)
     src_c = position // (ny * rows_dev)
     src_y = position // rows_dev % ny

time: 236 us -> 300 us (1.27)
  waiting for transfers between devices: 107 us -> 148 us
  blocking collectives: 15.8 us -> 32.9 us
  local copies, waits for them, and re-layouts: 15.8 us -> 19.5 us
    all_to_all x1, waiting for transfers between devices: 8.01 us -> 104 us  [shards(): lax.all_to_all(jnp.stack([centroids] * lax.axis_size(('z', 'x'))), ('z',...]
    all_gather x1, waiting for transfers between devices: 53.2 us -> 6.47 us  [shards(): lax.all_gather(embeddings, 'y', axis=0, tiled=True)]
    all_to_all x0 -> x1, blocking collectives: none -> 17.8 us  [shards(): lax.all_to_all(scores.reshape(devices, capacity), ALL, split_axis=0, conc...]
    all_gather x1 -> x0, waiting for transfers between devices: 15.8 us -> none  [shards(): piece = lax.all_gather(centroids, ('z', 'x'), axis=0, tiled=True)]
    all_to_all x1, waiting for transfers between devices: 25.5 us -> 33.1 us  [shards(): lax.all_to_all(outgoing.reshape(devices, capacity, feature_dim), ALL, spl...]
    another operation x0 -> x1, local copies, waits for them, and re-layouts: none -> 4.29 us  [shards(): jnp.stack([centroids] * lax.axis_size(('z', 'x')))]
  transfers between devices with their start and end apart: 6 -> 5, of which waited for: 5 -> 4; matrix products, arithmetic and copies ran while one was open for 16% -> 13% of each run, Pallas kernels for 0% -> 0%
where the time goes in v1:
time: 300 us
  waiting for transfers between devices  148 us (49%)
  matrix products  42.4 us (14%)
  blocking collectives  32.9 us (11%)
  starting transfers between devices  22.7 us (8%)
  local copies, waits for them, and re-layouts  19.5 us (6%)
  other arithmetic  18.5 us (6%)
  between operations  15.5 us (5%)
    all_to_all x1, waiting for transfers between devices, shards(): lax.all_to_all(jnp.stack([centroids] * lax.axis_size(('z', 'x'))), ('z',...  104 us
    dot_general x4, matrix products, step(): lax.dot_general(group, tile, (((1,), (1,)), ((), ())), preferred_element_...  38.8 us
    all_to_all x1, waiting for transfers between devices, shards(): lax.all_to_all(outgoing.reshape(devices, capacity, feature_dim), ALL, spl...  33.1 us
    all_to_all x1, blocking collectives, shards(): lax.all_to_all(scores.reshape(devices, capacity), ALL, split_axis=0, conc...  17.8 us
    pmax x1, blocking collectives, shards(): merged = lax.pmax(result, ('c', 'y'))  15.2 us
    neg x1, other arithmetic, gumbel_noise(): return -jnp.log(-jnp.log(uniform))  12.2 us
    all_to_all x1, starting transfers between devices, shards(): lax.all_to_all(present.reshape(devices, capacity), ALL, split_axis=0, con...  11.5 us
    all_gather x1, waiting for transfers between devices, shards(): lax.all_gather(embeddings, 'y', axis=0, tiled=True)  6.47 us
  transfers between devices with their start and end apart: 5, of which 4 were waited for; matrix products, arithmetic and copies ran while one was open for 13% of the time, Pallas kernels for 0%

profile of v1, /device:TPU:1, one launch (start us, length us, event | category | flops | bytes accessed | tf_op | source)
XLA Modules:
  0.0 300.0 jit_solution(4422752879383560562)
XLA Ops:
  7.2 0.0 all-gather.3.cloned.1.call-start
  7.2 0.7 all-gather.3.cloned.1.call-update
  7.9 0.9 convert_reduce_fusion
  8.8 0.7 compare_select_fusion
  9.5 2.2 scatter_custom_fusion
  11.7 0.8 all_to_all.21
  12.4 11.5 %all-to-all-start.1 = ((bf16[128,1,4]{2,1,0:T(2,128)(2,1)}), bf16[128,1,4]{2,1,0:T(2,128)(2,1)S(1)}, u32[]{:S(2)}, u32[]{:S(2)}) async-start(bf16[128,1,4]{2,1,0:T(2,128)(2,1)} %all_to_all.21), calls=%async_computation.1 | async-start | bytes 131072 | tf_op jit(solution)/shard_map/all_to_all | solution.py:106
  23.9 3.6 %scatter_custom_fusion.1 = bf16[512,2048]{1,0:T(8,128)(2,1)S(1)} fusion(s32[256]{0:T(256)S(1)} %bitcast.33, bf16[256,2048]{1,0:T(8,128)(2,1)} %param.6, bf16[]{:T(256)} %constant.177.clone.1), kind=kCustom, calls=%fused_computation.31 | custom fusion | bytes 2097664 | tf_op jit(solution)/shard_map/scatter | solution.py:93
  27.6 2.2 reshape.215
  29.8 3.7 %all-to-all-done.1 = bf16[128,1,4]{2,1,0:T(2,128)(2,1)S(1)} async-done(((bf16[128,1,4]{2,1,0:T(2,128)(2,1)}), bf16[128,1,4]{2,1,0:T(2,128)(2,1)S(1)}, u32[]{:S(2)}, u32[]{:S(2)}) %all-to-all-start.1) | async-done | bytes 1056 | tf_op jit(solution)/shard_map/all_to_all | solution.py:106
  33.4 6.1 %all-to-all-start.2 = ((bf16[128,4,2048]{2,1,0:T(4,128)(2,1)}), bf16[128,4,2048]{2,1,0:T(4,128)(2,1)S(1)}, u32[]{:S(2)}, u32[]{:S(2)}) async-start(bf16[128,4,2048]{2,1,0:T(4,128)(2,1)} %reshape.215), calls=%async_computation.2 | async-start | bytes 4194304 | tf_op jit(solution)/shard_map/all_to_all | solution.py:99
  39.6 0.0 all-gather.5.cloned.1.call-start
  39.6 0.3 broadcast_compare_fusion
  39.9 0.1 gt.22
  40.0 0.1 copy.15
  40.1 0.1 copy.16
  40.2 0.2 fusion.23
  40.4 33.1 %all-to-all-done.2 = bf16[128,4,2048]{2,1,0:T(4,128)(2,1)S(1)} async-done(((bf16[128,4,2048]{2,1,0:T(4,128)(2,1)}), bf16[128,4,2048]{2,1,0:T(4,128)(2,1)S(1)}, u32[]{:S(2)}, u32[]{:S(2)}) %all-to-all-start.2) | async-done | bytes 2097184 | tf_op jit(solution)/shard_map/all_to_all | solution.py:99
  73.5 2.1 fusion.15
  75.7 0.1 rsqrt.18
  75.8 0.0 copy-start
  75.8 2.1 reshape.216
  77.9 6.5 %all-gather.3.cloned.1.call-done = bf16[1024,2048]{1,0:T(8,128)(2,1)} async-done(((bf16[256,2048]{1,0:T(8,128)(2,1)}), bf16[1024,2048]{1,0:T(8,128)(2,1)}) %all-gather.3.cloned.1.call-update) | async-done | bytes 4194320 | tf_op jit(solution)/shard_map/all_gather | solution.py:56
  84.3 0.0 all-gather.5.cloned.1.call-update
  84.4 3.6 %fusion.19 = f32[512]{0:T(512)S(1)} fusion(bf16[512,2048]{1,0:T(8,128)(2,1)} %reshape.216, f32[512]{0:T(512)S(1)} %rsqrt.18, pred[512]{0:T(512)(128)(4,1)S(1)} %gt.22), kind=kOutput, calls=%fused_computation.30 | convolution fusion | flops 1075576320 | bytes 2101760 | tf_op jit(solution)/shard_map/dot_general | solution.py:33
  88.0 0.1 select_n.110
  88.1 17.8 %all_to_all.26 = f32[128,1,4]{2,1,0:T(1,128)S(1)} all-to-all(f32[128,1,4]{2,1,0:T(1,128)S(1)} %bitcast.29), channel_id=1, replica_groups=mesh['y'=4,'z'=4,'x'=4,'c'=2] {'y','z','x','c'}, dimensions={0} | all-to-all | bytes 4096 | tf_op jit(solution)/shard_map/all_to_all | solution.py:112
  105.9 0.0 copy-done
  105.9 4.3 %stack.2 = bf16[16,128,2048]{2,1,0:T(8,128)(2,1)} broadcast(bf16[128,2048]{1,0:T(8,128)(2,1)S(1)} %copy-done), dimensions={1,2} | broadcast | bytes 8912896 | tf_op jit(solution)/shard_map/stack | solution.py:59
  110.1 5.0 %all-to-all-start = ((bf16[16,128,2048]{2,1,0:T(8,128)(2,1)}), bf16[16,128,2048]{2,1,0:T(8,128)(2,1)}, u32[]{:S(2)}, u32[]{:S(2)}) async-start(bf16[16,128,2048]{2,1,0:T(8,128)(2,1)} %stack.2), calls=%async_computation | async-start | bytes 16777216 | tf_op jit(solution)/shard_map/all_to_all | solution.py:59
  115.9 12.2 %fusion.13 = f32[4,2048,512]{1,2,0:T(8,128)} fusion(s32[]{:T(128)} %bitcast.28, s32[4,512]{1,0:T(4,128)S(1)} %fusion.55, s32[2048]{0:T(1024)S(1)} %fusion.40), kind=kLoop, calls=%fused_computation.21 | loop fusion | flops 67108864 | bytes 16793604 | tf_op jit(solution)/shard_map/neg | solution.py:26
  128.1 0.6 multiply_reduce_fusion
  129.4 0.6 broadcast_multiply_fusion
  130.0 0.5 broadcast.397
  130.5 0.8 reduce.7
  131.3 0.1 reshape.217
  131.4 2.5 gather_fusion
  133.9 104.4 %all-to-all-done = bf16[16,128,2048]{2,1,0:T(8,128)(2,1)} async-done(((bf16[16,128,2048]{2,1,0:T(8,128)(2,1)}), bf16[16,128,2048]{2,1,0:T(8,128)(2,1)}, u32[]{:S(2)}, u32[]{:S(2)}) %all-to-all-start) | async-done | bytes 8388640 | tf_op jit(solution)/shard_map/all_to_all | solution.py:59
  238.4 0.0 all-gather.5.cloned.1.call-done
  238.4 39.0 %while.11 = (s32[]{:T(128)}, f32[2048]{0:T(1024)S(1)}, bf16[4,512,2048]{2,1,0:T(8,128)(2,1)}, bf16[2048,2048]{1,0:T(8,128)(2,1)}, f32[4,2048,512]{1,2,0:T(8,128)}, /*index=5*/s32[]{:T(128)}, s32[]{:T(128)}) while((s32[]{:T(128)}, f32[2048]{0:T(1024)S(1)}, bf16[4,512,2048]{2,1,0:T(8,128)(2,1)}, bf16[2048,2048]{1,0:T(8,128)(2,1)}, ...), condition=%wide.region_2.3_spmd.clone, body=%wide.region_0.2_spmd.clone.sunk | while | flops 4298115072 | bytes 14713951 | solution.py:85
  238.4 9.7 %fusion.69 = f32[2048]{0:T(1024)S(1)} fusion(f32[4,2048,512]{1,2,0:T(8,128)} %get-tuple-element.112, s32[]{:T(128)S(6)} %copy.19, bf16[2048,2048]{1,0:T(8,128)(2,1)} %get-tuple-element.111, bf16[4,512,2048]{2,1,0:T(8,128)(2,1)} %get-tuple-element.110), kind=kOutput, calls=%fused_computation.4.clone.1 | convolution fusion | flops 4298110976 | bytes 14689280 | tf_op jit(solution)/shard_map/while/body/eval_jaxpr/dot_general | solution.py:79
  248.1 9.7 %fusion.69 = f32[2048]{0:T(1024)S(1)} fusion(f32[4,2048,512]{1,2,0:T(8,128)} %get-tuple-element.112, s32[]{:T(128)S(6)} %copy.19, bf16[2048,2048]{1,0:T(8,128)(2,1)} %get-tuple-element.111, bf16[4,512,2048]{2,1,0:T(8,128)(2,1)} %get-tuple-element.110), kind=kOutput, calls=%fused_computation.4.clone.1 | convolution fusion | flops 4298110976 | bytes 14689280 | tf_op jit(solution)/shard_map/while/body/eval_jaxpr/dot_general | solution.py:79
  257.9 9.7 %fusion.69 = f32[2048]{0:T(1024)S(1)} fusion(f32[4,2048,512]{1,2,0:T(8,128)} %get-tuple-element.112, s32[]{:T(128)S(6)} %copy.19, bf16[2048,2048]{1,0:T(8,128)(2,1)} %get-tuple-element.111, bf16[4,512,2048]{2,1,0:T(8,128)(2,1)} %get-tuple-element.110), kind=kOutput, calls=%fused_computation.4.clone.1 | convolution fusion | flops 4298110976 | bytes 14689280 | tf_op jit(solution)/shard_map/while/body/eval_jaxpr/dot_general | solution.py:79
  267.6 9.7 %fusion.69 = f32[2048]{0:T(1024)S(1)} fusion(f32[4,2048,512]{1,2,0:T(8,128)} %get-tuple-element.112, s32[]{:T(128)S(6)} %copy.19, bf16[2048,2048]{1,0:T(8,128)(2,1)} %get-tuple-element.111, bf16[4,512,2048]{2,1,0:T(8,128)(2,1)} %get-tuple-element.110), kind=kOutput, calls=%fused_computation.4.clone.1 | convolution fusion | flops 4298110976 | bytes 14689280 | tf_op jit(solution)/shard_map/while/body/eval_jaxpr/dot_general | solution.py:79
  277.3 15.2 %pmax.7 = f32[2048]{0:T(1024)S(1)} all-reduce(f32[2048]{0:T(1024)S(1)} %get-tuple-element.30), channel_id=1, replica_groups=mesh['y'=4,'z'=4,'x'=4,'c'=2] {'c','y'}, use_global_device_ids=true, to_apply=%region_3.4 | all-reduce | flops 2048 | bytes 16384 | tf_op jit(solution)/shard_map/pmax | solution.py:86
  292.5 0.6 dynamic_slice.11
  (11 shorter events, 0.1 us)
Async XLA Ops:
  7.2 77.2 %all-gather.3.cloned.1.call-start = ((), (), s32[]{:S(2)}) async-start(), calls=%async_computation.4 | async-start | bytes 5242880 | tf_op jit(solution)/shard_map/all_gather | solution.py:56
  12.4 21.0 %all-to-all-start.1 = ((bf16[128,1,4]{2,1,0:T(2,128)(2,1)}), bf16[128,1,4]{2,1,0:T(2,128)(2,1)S(1)}, u32[]{:S(2)}, u32[]{:S(2)}) async-start(bf16[128,1,4]{2,1,0:T(2,128)(2,1)} %all_to_all.21), calls=%async_computation.1 | async-start | bytes 131072 | tf_op jit(solution)/shard_map/all_to_all | solution.py:106
  33.4 40.1 %all-to-all-start.2 = ((bf16[128,4,2048]{2,1,0:T(4,128)(2,1)}), bf16[128,4,2048]{2,1,0:T(4,128)(2,1)S(1)}, u32[]{:S(2)}, u32[]{:S(2)}) async-start(bf16[128,4,2048]{2,1,0:T(4,128)(2,1)} %reshape.215), calls=%async_computation.2 | async-start | bytes 4194304 | tf_op jit(solution)/shard_map/all_to_all | solution.py:99
  39.6 198.8 %all-gather.5.cloned.1.call-start = ((), (), s32[]{:S(2)}) async-start(), calls=%async_computation.5 | async-start | bytes 12582912 | tf_op jit(solution)/shard_map/all_gather | solution.py:55
  75.8 30.1 %copy-start = (bf16[128,2048]{1,0:T(8,128)(2,1)S(1)}, bf16[128,2048]{1,0:T(8,128)(2,1)}, u32[]{:S(2)}) copy-start(bf16[128,2048]{1,0:T(8,128)(2,1)} %param.7) | copy-start | bytes 1572868
  110.1 128.2 %all-to-all-start = ((bf16[16,128,2048]{2,1,0:T(8,128)(2,1)}), bf16[16,128,2048]{2,1,0:T(8,128)(2,1)}, u32[]{:S(2)}, u32[]{:S(2)}) async-start(bf16[16,128,2048]{2,1,0:T(8,128)(2,1)} %stack.2), calls=%async_computation | async-start | bytes 16777216 | tf_op jit(solution)/shard_map/all_to_all | solution.py:59
Sparse Core Ops, SparseCore 0:
  9.7 74.6 all-gather.2
  86.0 23.1 all-gather.4
